TPU v7x, 512 devices: a whole 4x8x8 slice. The times are simulated.
512 devices in a mesh: seq: 32 (over x, z), tp: 16 (over y, core).
Axes of the slice: x: 4, y: 8, z: 8, core: 2. Of those that a mesh axis runs over, the one named last changes fastest.
Arguments:
- residual: bfloat16 [6144, 8192], P('seq', 'tp'), may hold values from -6 to 6
- attention: bfloat16 [1536, 8192], P('seq'), may hold values from -6 to 6
- quantized_codes: int32 [8192, 8192], P('seq', 'tp'), may hold values from 0 to 15
- absmax: float32 [8192, 128], P('seq', 'tp'), may hold values from 0.005 to 0.05
- adapter_down: bfloat16 [8192, 64], P('seq'), may hold values from -0.0625 to 0.0625
- adapter_up: bfloat16 [64, 8192], P(None, 'tp'), may hold values from -0.75 to 0.75
- routed_slot_gate: float32 [1536], P('seq'), may hold values from 0.2 to 1
- selected: int32 [1536], P('seq'), may hold values from 0 to 191, as said below
- counts: int32 [32], P('seq'), may hold values from 1 to 48, 768 in all
- cotangent: bfloat16 [6144, 8192], P('seq', 'tp'), may hold values from -0.59765625 to 0.59765625
Outputs:
- outgoing_residual: bfloat16 [6144, 8192], P('seq', 'tp')
- attention_output_grad: bfloat16 [1536, 8192], P(None, 'seq')
- adapter_down_gradient: float32 [8192, 64], P('seq')
- adapter_up_gradient: float32 [64, 8192], P(None, 'tp')
- router_gate_gradient: float32 [1536], P('seq')
Inputs may be any that keep to these rules, and one draw needn't show every extreme that they name: `counts`: every shard has at least one live slot, all shards together have 768, and some shard has all 48 slots live. `selected`: within each shard's 48 slots the entries are distinct token positions of that shard; only the first counts entries of a shard are live.
All inputs are finite; a program needn't handle non-finite values.
Results may differ from a plain program's by a relative error of at most 0.0058.
Values may be sent and summed in bfloat16 or wider, within the bound.
A program may use at most 64 MiB of HBM per device.

v0:
```python
import jax
import jax.numpy as jnp
from jax import lax
from jax.sharding import PartitionSpec as P

LEVELS = (
    -1.0,
    -0.6961928009986877,
    -0.5250730514526367,
    -0.39491748809814453,
    -0.28444138169288635,
    -0.18477343022823334,
    -0.09105003625154495,
    0.0,
    0.07958029955625534,
    0.16093020141124725,
    0.24611230194568634,
    0.33791524171829224,
    0.44070982933044434,
    0.5626170039176941,
    0.7229568362236023,
    1.0,
)
adapter_scale = 0.25


def precise_matmul(left, right):
    return jnp.dot(left, right, precision=lax.Precision.HIGHEST, preferred_element_type=jnp.float32)


def dequantize(quantized_codes, absmax):
    quantile_levels = jnp.zeros(quantized_codes.shape, jnp.float32)
    for level_code in range(16):
        quantile_levels = quantile_levels + jnp.where(
            quantized_codes == level_code, LEVELS[level_code], 0.0
        )
    block_size = quantized_codes.shape[1] // absmax.shape[1]
    scales = jnp.repeat(absmax, block_size, axis=1)
    return (quantile_levels * scales).astype(jnp.bfloat16)


def body(
    residual,
    attention,
    quantized_codes,
    absmax,
    adapter_down,
    adapter_up,
    routed_slot_gate,
    selected,
    counts,
    cotangent,
):
    projection_weight = dequantize(quantized_codes, absmax)
    adapter_up_single32 = adapter_up.astype(jnp.float32)
    home_slots = attention.shape[0]
    live_slot = jnp.arange(home_slots, dtype=jnp.int32) < counts[0]
    target = jnp.where(live_slot, selected, residual.shape[0])
    full_w, full_a = (
        lax.all_gather(projection_weight, "seq", axis=0, tiled=True),
        lax.all_gather(adapter_down, "seq", axis=0, tiled=True),
    )
    adapter_product = jnp.dot(attention, full_a, preferred_element_type=jnp.float32)
    block_output = jnp.dot(
        attention, full_w, preferred_element_type=jnp.float32
    ) + adapter_scale * precise_matmul(adapter_product, adapter_up_single32)
    picked = residual[selected].astype(jnp.float32)
    updated = (picked + routed_slot_gate[:, None] * block_output).astype(jnp.bfloat16)
    outgoing_residual = residual.at[target].set(updated, mode="drop")
    upstream = jnp.where(live_slot[:, None], cotangent[selected].astype(jnp.float32), 0.0)
    gate_part = jnp.sum(upstream * block_output, axis=1)
    output_gradient = (routed_slot_gate[:, None] * upstream).astype(jnp.bfloat16)
    head_part = jnp.dot(output_gradient, full_w.T, preferred_element_type=jnp.float32)
    adapter_rank_piece = adapter_scale * jnp.dot(
        output_gradient, adapter_up.T, preferred_element_type=jnp.float32
    )
    head_full, rank_full, router_gate_gradient = lax.psum(
        (head_part, adapter_rank_piece, gate_part), "tp"
    )
    adapter_rank_gradient = rank_full.astype(jnp.bfloat16)
    home_grad = (
        head_full + jnp.dot(adapter_rank_gradient, full_a.T, preferred_element_type=jnp.float32)
    ).astype(jnp.bfloat16)
    attention_output_grad = lax.all_to_all(
        home_grad, "seq", split_axis=1, concat_axis=0, tiled=True
    )
    adapter_down_gradient = lax.psum_scatter(
        jnp.dot(attention.T, adapter_rank_gradient, preferred_element_type=jnp.float32),
        "seq",
        scatter_dimension=0,
        tiled=True,
    )
    up_factor_piece = adapter_scale * precise_matmul(
        adapter_product.T, output_gradient.astype(jnp.float32)
    )
    adapter_up_gradient = lax.psum(up_factor_piece, "seq")
    return (
        outgoing_residual,
        attention_output_grad,
        adapter_down_gradient,
        adapter_up_gradient,
        router_gate_gradient,
    )


def solution(mesh):
    return jax.shard_map(
        body,
        mesh=mesh,
        in_specs=(
            P("seq", "tp"),
            P("seq", None),
            P("seq", "tp"),
            P("seq", "tp"),
            P("seq", None),
            P(None, "tp"),
            P("seq"),
            P("seq"),
            P("seq"),
            P("seq", "tp"),
        ),
        out_specs=(P("seq", "tp"), P(None, "seq"), P("seq", None), P(None, "tp"), P("seq")),
        check_vma=False,
    )
```

profile of v0, /device:TPU:8, one launch (start us, length us, event | category | flops | bytes accessed | tf_op | source)
XLA Modules:
  0.0 714.8 jit_solution(8451295507987079360)
XLA Ops:
  7.3 1.3 copy.33
  8.6 2.2 fusion.2
  10.8 0.7 all-gather.5.cloned.1.call-update
  12.3 0.7 gather_fusion
  13.0 113.0 %all-gather.3.cloned.1.call-done = bf16[8192,512]{0,1:T(8,128)(2,1)} async-done(((bf16[256,512]{0,1:T(8,128)(2,1)}), bf16[8192,512]{0,1:T(8,128)(2,1)}) %all-gather.3.cloned.1.call-update) | async-done | bytes 8388624 | tf_op jit(solution)/shard_map/all_gather | solution.py:60
  126.0 6.1 fusion.8
  132.2 0.2 convolution_multiply_fusion.2
  132.4 71.0 %all-gather.5.cloned.1.call-done = bf16[8192,64]{0,1:T(8,128)(2,1)} async-done(((bf16[256,64]{0,1:T(8,128)(2,1)}), bf16[8192,64]{0,1:T(8,128)(2,1)}) %all-gather.5.cloned.1.call-update) | async-done | bytes 1048592 | tf_op jit(solution)/shard_map/all_gather | solution.py:61
  203.4 1.6 fusion.9
  205.1 0.9 convolution_multiply_fusion
  206.1 6.0 convolution_bitcast_fusion.1
  212.1 0.3 multiply_reduce_fusion
  212.4 42.8 %all-reduce = (bf16[48,64]{1,0:T(8,128)(2,1)S(1)}, f32[48]{0:T(128)}) all-reduce(f32[48,64]{1,0:T(8,128)S(1)} %convolution_multiply_fusion.2, f32[48]{0:T(128)S(1)} %get-tuple-element.9), channel_id=1, replica_groups=mesh['seq'=32,'tp'=16] {'tp'}, use_global_device_ids=true, to_apply=%region_2.3 | all-reduce | flops 3120 | bytes 18816 | tf_op jit(solution)/shard_map/psum | solution.py:77
  255.2 1.8 convolution_bitcast_fusion
  257.1 64.0 %all-reduce.4.cloned.1.call-done = f32[48,8192]{1,0:T(8,128)} async-done(((f32[48,8192]{1,0:T(8,128)}), f32[48,8192]{1,0:T(8,128)}) %all-reduce.4.cloned.1.call-update) | async-done | bytes 1572880 | tf_op jit(solution)/shard_map/psum | solution.py:77
  321.1 1.8 fusion
  322.9 0.9 copy.51
  323.8 9.3 %all-to-all-start = ((bf16[48,32,256]{2,0,1:T(8,128)(2,1)}), bf16[48,32,256]{2,0,1:T(8,128)(2,1)S(1)}, u32[]{:S(2)}, u32[]{:S(2)}) async-start(bf16[48,32,256]{2,0,1:T(8,128)(2,1)} %bitcast.28), calls=%async_computation | async-start | bytes 1572864 | tf_op jit(solution)/shard_map/all_to_all | solution.py:84
  333.1 1.2 scatter_custom_fusion
  334.3 23.0 %all-to-all-done = bf16[48,32,256]{2,0,1:T(8,128)(2,1)S(1)} async-done(((bf16[48,32,256]{2,0,1:T(8,128)(2,1)}), bf16[48,32,256]{2,0,1:T(8,128)(2,1)S(1)}, u32[]{:S(2)}, u32[]{:S(2)}) %all-to-all-start) | async-done | bytes 786464 | tf_op jit(solution)/shard_map/all_to_all | solution.py:84
  357.3 123.7 %all-reduce.6.cloned.1.call-done = f32[64,512]{1,0:T(8,128)} async-done(((f32[64,512]{1,0:T(8,128)}), f32[64,512]{1,0:T(8,128)}) %all-reduce.6.cloned.1.call-update) | async-done | bytes 131088 | tf_op jit(solution)/shard_map/psum | solution.py:96
  481.0 224.9 %reduce-scatter.2.cloned.1.call-done = f32[256,64]{0,1:T(8,128)} async-done(((f32[8192,64]{0,1:T(8,128)}), f32[256,64]{0,1:T(8,128)}) %reduce-scatter.2.cloned.1.call-update) | async-done | bytes 65552 | tf_op jit(solution)/shard_map/reduce_scatter | solution.py:87
  705.9 0.9 copy.59
  706.7 1.6 copy.60
  (28 shorter events, 0.3 us)
Async XLA Ops:
  7.2 196.3 %copy-start = (bf16[48,8192]{1,0:T(8,128)(2,1)S(1)}, bf16[48,8192]{1,0:T(8,128)(2,1)}, u32[]{:S(2)}) copy-start(bf16[48,8192]{1,0:T(8,128)(2,1)} %param.11) | copy-start | bytes 2359300
  7.2 5.1 copy-start.7
  7.2 5.1 copy-start.4
  7.2 118.8 %copy-start.6 = (f32[48]{0:T(128)S(1)}, f32[48]{0:T(128)}, u32[]{:S(2)}) copy-start(f32[48]{0:T(128)} %param.16) | copy-start | bytes 580
  7.2 118.8 %all-gather.3.cloned.1.call-start = ((), (), s32[]{:S(2)}) async-start(), calls=%async_computation.2 | async-start | bytes 8650752 | tf_op jit(solution)/shard_map/all_gather | solution.py:60
  10.8 192.6 %all-gather.5.cloned.1.call-start = ((), (), s32[]{:S(2)}) async-start(), calls=%async_computation.3 | async-start | bytes 1081344 | tf_op jit(solution)/shard_map/all_gather | solution.py:61
  11.5 309.5 %all-reduce.4.cloned.1.call-start = ((), (), s32[]{:S(2)}) async-start(), calls=%async_computation.4 | async-start | bytes 3145728 | tf_op jit(solution)/shard_map/psum | solution.py:77
  13.0 119.2 %copy-start.5 = (bf16[64,512]{1,0:T(8,128)(2,1)S(1)}, bf16[64,512]{1,0:T(8,128)(2,1)}, u32[]{:S(2)}) copy-start(bf16[64,512]{1,0:T(8,128)(2,1)} %param.15) | copy-start | bytes 196612
  132.1 348.8 %all-reduce.6.cloned.1.call-start = ((), (), s32[]{:S(2)}) async-start(), calls=%async_computation.6 | async-start | bytes 262144 | tf_op jit(solution)/shard_map/psum | solution.py:96
  206.0 499.8 %reduce-scatter.2.cloned.1.call-start = ((), (), s32[]{:S(2)}) async-start(), calls=%async_computation.5 | async-start | bytes 2162688 | tf_op jit(solution)/shard_map/reduce_scatter | solution.py:87
  255.2 65.8 %copy-start.1 = (bf16[8192,64]{0,1:T(8,128)(2,1)S(1)}, bf16[8192,64]{0,1:T(8,128)(2,1)}, u32[]{:S(2)}) copy-start(bf16[8192,64]{0,1:T(8,128)(2,1)} %all-gather.5.cloned.1.call-done) | copy-start | bytes 3145732
  322.8 10.2 %copy-start.3 = (bf16[192,512]{1,0:T(8,128)(2,1)S(1)}, bf16[192,512]{1,0:T(8,128)(2,1)}, u32[]{:S(2)}) copy-start(bf16[192,512]{1,0:T(8,128)(2,1)} %param.10) | copy-start | bytes 589828
  323.8 33.5 %all-to-all-start = ((bf16[48,32,256]{2,0,1:T(8,128)(2,1)}), bf16[48,32,256]{2,0,1:T(8,128)(2,1)S(1)}, u32[]{:S(2)}, u32[]{:S(2)}) async-start(bf16[48,32,256]{2,0,1:T(8,128)(2,1)} %bitcast.28), calls=%async_computation | async-start | bytes 1572864 | tf_op jit(solution)/shard_map/all_to_all | solution.py:84
  334.3 374.0 %copy-start.2 = (bf16[192,512]{1,0:T(8,128)(2,1)}, bf16[192,512]{1,0:T(8,128)(2,1)S(1)}, u32[]{:S(2)}) copy-start(bf16[192,512]{1,0:T(8,128)(2,1)S(1)} %scatter_custom_fusion) | copy-start | bytes 589828
Sparse Core Ops, SparseCore 0:
  11.7 114.2 all-gather.2
  129.0 74.3 all-gather.4
  205.8 115.2 all-reduce.3
  325.3 155.5 all-reduce.5
  485.8 220.0 reduce-scatter.1
where the time goes:
time: 715 us
  waiting for transfers between devices  620 us (87%)
  blocking collectives  42.8 us (6%)
  matrix products  18.8 us (3%)
  between operations  14.6 us (2%)
  starting transfers between devices  9.47 us (1%)
    reduce_scatter x1, waiting for transfers between devices, body(): lax.psum_scatter(jnp.dot(attention.T, adapter_rank_gradient, preferred_el...  225 us
    psum x1, waiting for transfers between devices, body(): adapter_up_gradient = lax.psum(up_factor_piece, 'seq')  124 us
    all_gather x1, waiting for transfers between devices, body(): lax.all_gather(projection_weight, 'seq', axis=0, tiled=True)  113 us
    all_gather x1, waiting for transfers between devices, body(): lax.all_gather(adapter_down, 'seq', axis=0, tiled=True)  71 us
    psum x1, waiting for transfers between devices, body(): lax.psum((head_part, adapter_rank_piece, gate_part), 'tp')  64 us
    psum x1, blocking collectives, body(): lax.psum((head_part, adapter_rank_piece, gate_part), 'tp')  42.8 us
    all_to_all x1, waiting for transfers between devices, body(): lax.all_to_all(home_grad, 'seq', split_axis=1, concat_axis=0, tiled=True)  23 us
  transfers between devices with their start and end apart: 6, of which 6 were waited for; matrix products, arithmetic and copies ran while one was open for 3% of the time, Pallas kernels for 0%

commit v1 on v0

--- a/solution.py
+++ b/solution.py
@@ -81,9 +81,13 @@
     home_grad = (
         head_full + jnp.dot(adapter_rank_gradient, full_a.T, preferred_element_type=jnp.float32)
     ).astype(jnp.bfloat16)
-    attention_output_grad = lax.all_to_all(
-        home_grad, "seq", split_axis=1, concat_axis=0, tiled=True
+    order_the_rates = lambda block_here, axis_id, axis_no, array_dim: jnp.concatenate(
+        lax.all_to_all(
+            jnp.stack(jnp.split(block_here, lax.axis_size(axis_id), axis=axis_no)), axis_id, 0, 0
+        ),
+        array_dim,
     )
+    attention_output_grad = order_the_rates(home_grad, axis_id="seq", axis_no=1, array_dim=0)
     adapter_down_gradient = lax.psum_scatter(
         jnp.dot(attention.T, adapter_rank_gradient, preferred_element_type=jnp.float32),
         "seq",

time: 715 us -> 718 us (level)
  local copies, waits for them, and re-layouts: 5.41 us -> 24 us
  waiting for transfers between devices: 620 us -> 604 us
    unnamed x19 -> x50, local copies, waits for them, and re-layouts: 3.81 us -> 22.8 us
    psum x1, waiting for transfers between devices: 124 us -> 108 us  [body(): adapter_up_gradient = lax.psum(up_factor_piece, 'seq')]
  transfers between devices with their start and end apart: 6 -> 6, of which waited for: 6 -> 6; matrix products, arithmetic and copies ran while one was open for 3% -> 6% of each run, Pallas kernels for 0% -> 0%
where the time goes in v1:
time: 718 us; the launch traced here: 717 us
  waiting for transfers between devices  604 us (84%)
  blocking collectives  42.8 us (6%)
  local copies, waits for them, and re-layouts  24 us (3%)
  matrix products  18.8 us (3%)
  between operations  14.6 us (2%)
  starting transfers between devices  9.47 us (1%)
    reduce_scatter x1, waiting for transfers between devices, body(): lax.psum_scatter(jnp.dot(attention.T, adapter_rank_gradient, preferred_el...  225 us
    all_gather x1, waiting for transfers between devices, body(): lax.all_gather(projection_weight, 'seq', axis=0, tiled=True)  113 us
    psum x1, waiting for transfers between devices, body(): adapter_up_gradient = lax.psum(up_factor_piece, 'seq')  108 us
    all_gather x1, waiting for transfers between devices, body(): lax.all_gather(adapter_down, 'seq', axis=0, tiled=True)  71 us
    psum x1, waiting for transfers between devices, body(): lax.psum((head_part, adapter_rank_piece, gate_part), 'tp')  64 us
    psum x1, blocking collectives, body(): lax.psum((head_part, adapter_rank_piece, gate_part), 'tp')  42.8 us
    unnamed x50, local copies, waits for them, and re-layouts  22.8 us
    all_to_all x1, waiting for transfers between devices, body(): lax.all_to_all(jnp.stack(jnp.split(block_here, lax.axis_size(axis_id), ax...  22.5 us
  transfers between devices with their start and end apart: 6, of which 6 were waited for; matrix products, arithmetic and copies ran while one was open for 6% of the time, Pallas kernels for 0%

profile of v1, /device:TPU:8, one launch (start us, length us, event | category | flops | bytes accessed | tf_op | source)
XLA Modules:
  0.0 717.3 jit_solution(18225648584615811446)
XLA Ops:
  7.3 1.3 copy.16
  8.6 2.2 fusion.2
  10.8 0.7 all-gather.5.cloned.1.call-update
  12.3 0.7 gather_fusion
  13.0 113.0 %all-gather.3.cloned.1.call-done = bf16[8192,512]{0,1:T(8,128)(2,1)} async-done(((bf16[256,512]{0,1:T(8,128)(2,1)}), bf16[8192,512]{0,1:T(8,128)(2,1)}) %all-gather.3.cloned.1.call-update) | async-done | bytes 8388624 | tf_op jit(solution)/shard_map/all_gather | solution.py:60
  126.0 6.1 fusion.8
  132.4 71.0 %all-gather.5.cloned.1.call-done = bf16[8192,64]{0,1:T(8,128)(2,1)} async-done(((bf16[256,64]{0,1:T(8,128)(2,1)}), bf16[8192,64]{0,1:T(8,128)(2,1)}) %all-gather.5.cloned.1.call-update) | async-done | bytes 1048592 | tf_op jit(solution)/shard_map/all_gather | solution.py:61
  203.4 1.6 fusion.9
  205.1 0.9 convolution_multiply_fusion
  206.1 6.0 convolution_bitcast_fusion.1
  212.4 42.8 %all-reduce = (bf16[48,64]{1,0:T(8,128)(2,1)S(1)}, f32[48]{0:T(128)}) all-reduce(f32[48,64]{1,0:T(8,128)S(1)} %convolution_multiply_fusion.2, f32[48]{0:T(128)S(1)} %get-tuple-element.9), channel_id=1, replica_groups=mesh['seq'=32,'tp'=16] {'tp'}, use_global_device_ids=true, to_apply=%region_2.3 | all-reduce | flops 3120 | bytes 18816 | tf_op jit(solution)/shard_map/psum | solution.py:77
  255.2 1.8 convolution_bitcast_fusion
  257.1 64.0 %all-reduce.4.cloned.1.call-done = f32[48,8192]{1,0:T(8,128)} async-done(((f32[48,8192]{1,0:T(8,128)}), f32[48,8192]{1,0:T(8,128)}) %all-reduce.4.cloned.1.call-update) | async-done | bytes 1572880 | tf_op jit(solution)/shard_map/psum | solution.py:77
  321.1 1.8 fusion
  322.9 0.6 constant_dynamic-update-slice_fusion.31
  323.5 0.6 constant_dynamic-update-slice_fusion.30
  324.1 0.6 constant_dynamic-update-slice_fusion.29
  342.4 9.3 %all-to-all-start = ((bf16[32,48,256]{2,1,0:T(8,128)(2,1)}), bf16[32,48,256]{2,1,0:T(8,128)(2,1)S(1)}, u32[]{:S(2)}, u32[]{:S(2)}) async-start(bf16[32,48,256]{2,1,0:T(8,128)(2,1)} %constant_dynamic-update-slice_fusion), calls=%async_computation | async-start | bytes 1572864 | tf_op jit(solution)/shard_map/all_to_all | solution.py:85
  351.7 1.2 scatter_custom_fusion
  352.9 22.5 %all-to-all-done = bf16[32,48,256]{2,1,0:T(8,128)(2,1)S(1)} async-done(((bf16[32,48,256]{2,1,0:T(8,128)(2,1)}), bf16[32,48,256]{2,1,0:T(8,128)(2,1)S(1)}, u32[]{:S(2)}, u32[]{:S(2)}) %all-to-all-start) | async-done | bytes 786464 | tf_op jit(solution)/shard_map/all_to_all | solution.py:85
  375.5 108.0 %all-reduce.6.cloned.1.call-done = f32[64,512]{1,0:T(8,128)} async-done(((f32[64,512]{1,0:T(8,128)}), f32[64,512]{1,0:T(8,128)}) %all-reduce.6.cloned.1.call-update) | async-done | bytes 131088 | tf_op jit(solution)/shard_map/psum | solution.py:100
  483.5 224.9 %reduce-scatter.2.cloned.1.call-done = f32[256,64]{0,1:T(8,128)} async-done(((f32[8192,64]{0,1:T(8,128)}), f32[256,64]{0,1:T(8,128)}) %reduce-scatter.2.cloned.1.call-update) | async-done | bytes 65552 | tf_op jit(solution)/shard_map/reduce_scatter | solution.py:91
  708.4 0.9 copy.69
  709.2 1.6 copy.70
  (59 shorter events, 18.5 us)
Async XLA Ops:
  7.2 196.3 %copy-start = (bf16[48,8192]{1,0:T(8,128)(2,1)S(1)}, bf16[48,8192]{1,0:T(8,128)(2,1)}, u32[]{:S(2)}) copy-start(bf16[48,8192]{1,0:T(8,128)(2,1)} %param.11) | copy-start | bytes 2359300
  7.2 5.1 copy-start.7
  7.2 5.1 copy-start.4
  7.2 118.8 %copy-start.6 = (f32[48]{0:T(128)S(1)}, f32[48]{0:T(128)}, u32[]{:S(2)}) copy-start(f32[48]{0:T(128)} %param.16) | copy-start | bytes 580
  7.2 118.8 %all-gather.3.cloned.1.call-start = ((), (), s32[]{:S(2)}) async-start(), calls=%async_computation.2 | async-start | bytes 8650752 | tf_op jit(solution)/shard_map/all_gather | solution.py:60
  10.8 192.6 %all-gather.5.cloned.1.call-start = ((), (), s32[]{:S(2)}) async-start(), calls=%async_computation.3 | async-start | bytes 1081344 | tf_op jit(solution)/shard_map/all_gather | solution.py:61
  11.5 309.5 %all-reduce.4.cloned.1.call-start = ((), (), s32[]{:S(2)}) async-start(), calls=%async_computation.4 | async-start | bytes 3145728 | tf_op jit(solution)/shard_map/psum | solution.py:77
  13.0 119.2 %copy-start.5 = (bf16[64,512]{1,0:T(8,128)(2,1)S(1)}, bf16[64,512]{1,0:T(8,128)(2,1)}, u32[]{:S(2)}) copy-start(bf16[64,512]{1,0:T(8,128)(2,1)} %param.15) | copy-start | bytes 196612
  132.1 351.3 %all-reduce.6.cloned.1.call-start = ((), (), s32[]{:S(2)}) async-start(), calls=%async_computation.6 | async-start | bytes 262144 | tf_op jit(solution)/shard_map/psum | solution.py:100
  206.0 502.3 %reduce-scatter.2.cloned.1.call-start = ((), (), s32[]{:S(2)}) async-start(), calls=%async_computation.5 | async-start | bytes 2162688 | tf_op jit(solution)/shard_map/reduce_scatter | solution.py:91
  255.2 65.8 %copy-start.1 = (bf16[8192,64]{0,1:T(8,128)(2,1)S(1)}, bf16[8192,64]{0,1:T(8,128)(2,1)}, u32[]{:S(2)}) copy-start(bf16[8192,64]{0,1:T(8,128)(2,1)} %all-gather.5.cloned.1.call-done) | copy-start | bytes 3145732
  322.8 28.9 %copy-start.3 = (bf16[192,512]{1,0:T(8,128)(2,1)S(1)}, bf16[192,512]{1,0:T(8,128)(2,1)}, u32[]{:S(2)}) copy-start(bf16[192,512]{1,0:T(8,128)(2,1)} %param.10) | copy-start | bytes 589828
  342.4 33.0 %all-to-all-start = ((bf16[32,48,256]{2,1,0:T(8,128)(2,1)}), bf16[32,48,256]{2,1,0:T(8,128)(2,1)S(1)}, u32[]{:S(2)}, u32[]{:S(2)}) async-start(bf16[32,48,256]{2,1,0:T(8,128)(2,1)} %constant_dynamic-update-slice_fusion), calls=%async_computation | async-start | bytes 1572864 | tf_op jit(solution)/shard_map/all_to_all | solution.py:85
  352.9 357.9 %copy-start.2 = (bf16[192,512]{1,0:T(8,128)(2,1)}, bf16[192,512]{1,0:T(8,128)(2,1)S(1)}, u32[]{:S(2)}) copy-start(bf16[192,512]{1,0:T(8,128)(2,1)S(1)} %scatter_custom_fusion) | copy-start | bytes 589828
Sparse Core Ops, SparseCore 0:
  11.7 114.2 all-gather.2
  129.0 74.3 all-gather.4
  205.8 115.2 all-reduce.3
  325.3 158.0 all-reduce.5
  488.3 220.0 reduce-scatter.1
